TPU v7x, 128 devices: a whole 4x4x4 slice. The times are simulated.
128 devices in a mesh: dp: 16 (over z, x), expert: 8 (over y, core).
Axes of the slice: x: 4, y: 4, z: 4, core: 2. Of those that a mesh axis runs over, the one named last changes fastest.
Arguments:
- tokens: bfloat16 [32768, 1536], P(('dp', 'expert')), may hold values from -6 to 6
- attn_gain: float32 [1536], replicated, may hold values from 0.1 to 1.9
- ffn_gain: float32 [1536], replicated, may hold values from 0.1 to 1.9
- w_query: bfloat16 [1536, 1536], replicated, may hold values from -0.15625 to 0.15625
- w_key: bfloat16 [1536, 256], replicated, may hold values from -0.15625 to 0.15625
- w_value: bfloat16 [1536, 256], replicated, may hold values from -0.15625 to 0.15625
- w_out: bfloat16 [1536, 1536], replicated, may hold values from -0.15625 to 0.15625
- key_cache: bfloat16 [384, 2048, 256], P(('dp', 'expert')), may hold values from -200 to 200
- value_cache: bfloat16 [384, 2048, 256], P(('dp', 'expert')), may hold values from -6 to 6
- req_lengths: int32 [128, 3], P(('dp', 'expert')), may hold values from 1 to 128, 256 in all within a row
- cache_lengths: int32 [128, 3], P(('dp', 'expert')), may hold values from 1024 to 2048
- expert_ids: int32 [32768, 4], P(('dp', 'expert')), may hold values from 0 to 31, all different within a row; in each aligned block of 32 rows (0 to 31, 32 to 63, ...) at most 8 rows name the same one
- route_gate: float32 [32768, 4], P(('dp', 'expert')), may hold values from 0.1 to 1
- replica_owner: int32 [32, 8], replicated, may hold values from 0 to 7, each once within a row
- replica_pick: int32 [128, 8], P(('dp', 'expert')), may hold values from 0 to 7, each once within a row
- w_gate_up: bfloat16 [32, 768, 2, 1536], P('dp', 'expert'), may hold values from -0.15625 to 0.15625
- w_down: bfloat16 [32, 1536, 768], P('dp', 'expert'), may hold values from -0.21875 to 0.21875
Outputs:
- layer_out: bfloat16 [32768, 1536], P(('dp', 'expert'))
- owner_rows: int32 [128, 2], P(('dp', 'expert'))
Inputs may be any that keep to these rules, and one draw needn't show every extreme that they name: `req_lengths`: a row holds one device's request lengths in the order of its tokens; it sums to 256 and its largest is 128. `expert_ids`: a token's 4 ids differ; in each aligned block of 32 tokens no expert is named more than 8 times. `replica_owner`: each expert's row names every index of the expert axis once. `replica_pick`: each device's row names every replica once.
All inputs are finite; a program needn't handle non-finite values.
Results may differ from a plain program's by a relative error of at most 0.015.
Values may be sent and summed in bfloat16 or wider, within the bound.
A program may use at most 192 MiB of HBM per device.

v0:
```python
import jax
import jax.numpy as jnp
from jax import lax
from jax.experimental import pallas as pl
from jax.experimental.pallas import tpu as pltpu
from jax.sharding import PartitionSpec as P

HEADS = 12
KV_HEADS = 2
HEAD_DIM = 128


epsilon = 1e-06
rope_base = 1000000.0


GROUP = HEADS // KV_HEADS
TILE = 64
CACHE = 2048
OPEN = 1024


def front_kernel(
    lengths_ref,
    cached_ref,
    pick_ref,
    tokens_ref,
    attn_gain_ref,
    ffn_gain_ref,
    inverse_ref,
    ids_ref,
    gate_ref,
    owners_ref,
    w_query_hbm,
    w_key_hbm,
    w_value_hbm,
    w_out_hbm,
    keys_hbm,
    values_hbm,
    residual_ref,
    normed_ref,
    table_ref,
    counts_ref,
    w_query,
    w_key,
    w_value,
    w_out,
    keys,
    values,
    new_keys,
    new_values,
    queries,
    attended,
    sem_w,
    sem_k,
    sem_v,
):
    count = tokens_ref.shape[0]
    loads = [
        pltpu.make_async_copy(w_query_hbm, w_query, sem_w.at[0]),
        pltpu.make_async_copy(w_key_hbm, w_key, sem_w.at[1]),
        pltpu.make_async_copy(w_value_hbm, w_value, sem_w.at[2]),
    ]

    def cache_loads(request):
        copies = []
        for group in range(KV_HEADS):
            lanes = pl.ds(group * HEAD_DIM, HEAD_DIM)
            copies.append(
                pltpu.make_async_copy(
                    keys_hbm.at[request, :, lanes], keys.at[request, group], sem_k.at[request, group]
                )
            )
            copies.append(
                pltpu.make_async_copy(
                    values_hbm.at[request, :, lanes],
                    values.at[request, group, :, pl.ds(0, HEAD_DIM)],
                    sem_v.at[request, group],
                )
            )
        return copies

    last_load = pltpu.make_async_copy(w_out_hbm, w_out, sem_w.at[3])
    for copy in loads:
        copy.start()
    for request in range(3):
        for copy in cache_loads(request):
            copy.start()
    last_load.start()

    starts = [0, lengths_ref[0, 0], lengths_ref[0, 0] + lengths_ref[0, 1]]
    ends = [starts[1], starts[2], count]
    cached = [cached_ref[0, request] for request in range(3)]

    def by_request(token, values_of):
        return jnp.where(
            token < starts[1], values_of[0], jnp.where(token < starts[2], values_of[1], values_of[2])
        )

    lane = lax.broadcasted_iota(jnp.int32, (count, 128), 1)
    row = lax.broadcasted_iota(jnp.int32, (count, 128), 0)
    hots = [(ids_ref[:, k : k + 1] == lane).astype(jnp.float32) for k in range(4)]
    hot = hots[0] + hots[1] + hots[2] + hots[3]
    later = lax.broadcasted_iota(jnp.int32, (count, count), 0)
    sooner = lax.broadcasted_iota(jnp.int32, (count, count), 1)
    before = jnp.dot(
        ((later // 32 == sooner // 32) & (sooner < later)).astype(jnp.float32).astype(jnp.bfloat16),
        hot.astype(jnp.bfloat16),
        preferred_element_type=jnp.float32,
    )
    columns = jnp.zeros((count, 128), jnp.float32)
    for k in range(4):
        rank = jnp.sum(hots[k] * before, axis=1, keepdims=True)
        code = (ids_ref[:, k : k + 1] * 32).astype(jnp.float32) + rank
        columns = jnp.where(lane == k, code, columns)
        columns = jnp.where(lane == 4 + k, gate_ref[:, k : k + 1], columns)
    columns = columns + jnp.where(lane < 4, ((row // 32) % 4 * 8).astype(jnp.float32), 0.0)
    table_ref[...] = columns.T[0:8, :]

    blocks = lax.broadcasted_iota(jnp.int32, (8, count), 0)
    members = lax.broadcasted_iota(jnp.int32, (8, count), 1)
    per_block = jnp.dot(
        (members // 32 == blocks).astype(jnp.float32).astype(jnp.bfloat16),
        hot.astype(jnp.bfloat16),
        preferred_element_type=jnp.float32,
    )
    place_of = lax.broadcasted_iota(jnp.int32, (8, 128), 0)
    per_owner = jnp.zeros((8, 128), jnp.float32)
    for block in range(8):
        owner = owners_ref[pl.ds(pick_ref[0, block], 1), :]
        per_owner = per_owner + jnp.where(place_of == owner, per_block[block : block + 1, :], 0.0)
    expert_row = lax.broadcasted_iota(jnp.int32, (128, 128), 0)
    owner_lane = lax.broadcasted_iota(jnp.int32, (128, 128), 1)
    tallied = jnp.zeros((8, 128), jnp.float32)
    for j in range(2):
        moved = jnp.dot(
            per_owner.astype(jnp.bfloat16),
            (expert_row == owner_lane // 8 * 2 + j).astype(jnp.float32).astype(jnp.bfloat16),
            preferred_element_type=jnp.float32,
        )
        own = jnp.sum(
            jnp.where(lax.broadcasted_iota(jnp.int32, (8, 128), 1) % 8 == place_of, moved, 0.0),
            axis=0,
            keepdims=True,
        )
        tallied = jnp.where(place_of == j, own, tallied)
    counts_ref[...] = tallied.astype(jnp.int32)

    for request in range(3):
        for group in range(KV_HEADS):
            values[request, group, :, HEAD_DIM:] = jnp.ones((CACHE, HEAD_DIM), jnp.bfloat16)
    for group in range(KV_HEADS):
        new_values[group, :, HEAD_DIM:] = jnp.ones((count, HEAD_DIM), jnp.bfloat16)

    wide = tokens_ref[...].astype(jnp.float32)
    scale = lax.rsqrt(jnp.mean(wide * wide, axis=1, keepdims=True) + epsilon)
    normed = (wide * scale * attn_gain_ref[...]).astype(jnp.bfloat16)

    position = row + by_request(row, [cached[0], cached[1] - starts[1], cached[2] - starts[2]])
    angle = position.astype(jnp.float32) * inverse_ref[...]
    cosine = jnp.cos(angle)
    sine = jnp.sin(angle)
    sine = jnp.where(lane < HEAD_DIM // 2, -sine, sine)

    def turned(head):
        return (head * cosine + pltpu.roll(head, HEAD_DIM // 2, 1) * sine).astype(jnp.bfloat16)

    loads[0].wait()
    for part in range(HEADS // 2):
        pair = jnp.dot(
            normed,
            w_query[:, part * 256 : (part + 1) * 256],
            preferred_element_type=jnp.float32,
        )
        for side in range(2):
            queries[part * 2 + side] = turned(pair[:, side * HEAD_DIM : (side + 1) * HEAD_DIM])
    loads[1].wait()
    fresh_keys = jnp.dot(normed, w_key[...], preferred_element_type=jnp.float32)
    loads[2].wait()
    fresh_values = jnp.dot(normed, w_value[...], preferred_element_type=jnp.float32)
    for group in range(KV_HEADS):
        lanes = slice(group * HEAD_DIM, (group + 1) * HEAD_DIM)
        new_keys[group] = turned(fresh_keys[:, lanes])
        new_values[group, :, 0:HEAD_DIM] = fresh_values[:, lanes].astype(jnp.bfloat16)

    factor = HEAD_DIM ** (-0.5) * 1.4426950408889634
    stack = GROUP * TILE
    last = (((1,), (1,)), ((), ()))
    lowest = -jnp.inf
    for request in range(3):
        for copy in cache_loads(request):
            copy.wait()
        start, end, filled = starts[request], ends[request], cached[request]

        def attend(tile, carry, request=request, start=start, end=end, filled=filled):
            base = pl.multiple_of(tile * TILE, TILE)
            token = base + lax.broadcasted_iota(jnp.int32, (stack, 128), 0) % TILE
            here = filled + token - start
            slot = lax.broadcasted_iota(jnp.int32, (stack, 128), 1)
            near = (slot == 0) | (here - slot < CACHE)
            open_slot = OPEN + lax.broadcasted_iota(jnp.int32, (1, CACHE - OPEN), 1)
            bias = jnp.where(open_slot < filled, 0.0, lowest)
            fresh = lax.broadcasted_iota(jnp.int32, (stack, count), 1)
            asking = base + lax.broadcasted_iota(jnp.int32, (stack, count), 0) % TILE
            seen = (fresh >= start) & (fresh <= asking)
            inside = (token >= start) & (token < end)
            for group in range(KV_HEADS):
                asked = queries[group * GROUP : (group + 1) * GROUP, pl.ds(base, TILE), :].reshape(
                    stack, HEAD_DIM
                )

                def score(block):
                    return lax.dot_general(asked, block, last, preferred_element_type=jnp.float32)

                parts = [
                    jnp.where(near, score(keys[request, group, 0:128, :]), lowest),
                    score(keys[request, group, 128:OPEN, :]),
                    score(keys[request, group, OPEN:CACHE, :]) + bias,
                    jnp.where(seen, score(new_keys[group]), lowest),
                ]
                peak = jnp.max(parts[0], axis=1, keepdims=True)
                for part in parts[1:]:
                    peak = jnp.maximum(peak, jnp.max(part, axis=1, keepdims=True))
                peak = peak * factor
                blocks = [
                    values[request, group, 0:128, :],
                    values[request, group, 128:OPEN, :],
                    values[request, group, OPEN:CACHE, :],
                    new_values[group],
                ]
                mixed = jnp.zeros((stack, 2 * HEAD_DIM), jnp.float32)
                for part, block in zip(parts, blocks):
                    weight = jnp.exp2(part * factor - peak).astype(jnp.bfloat16)
                    mixed = mixed + jnp.dot(weight, block, preferred_element_type=jnp.float32)
                answer = mixed[:, 0:HEAD_DIM] / mixed[:, HEAD_DIM:]
                for member in range(GROUP):
                    rows = slice(member * TILE, (member + 1) * TILE)
                    head = group * GROUP + member
                    spot = (pl.ds(base, TILE), slice(head * HEAD_DIM, (head + 1) * HEAD_DIM))
                    kept = attended[spot].astype(jnp.float32)
                    attended[spot] = jnp.where(inside[rows], answer[rows], kept).astype(jnp.bfloat16)
            return carry

        lax.fori_loop(start // TILE, (end + TILE - 1) // TILE, attend, 0)

    last_load.wait()
    projected = jnp.dot(attended[...], w_out[...], preferred_element_type=jnp.float32)
    residual = (tokens_ref[...].astype(jnp.float32) + projected).astype(jnp.bfloat16)
    residual_ref[...] = residual
    wide = residual.astype(jnp.float32)
    scale = lax.rsqrt(jnp.mean(wide * wide, axis=1, keepdims=True) + epsilon)
    normed_ref[...] = (wide * scale * ffn_gain_ref[...]).astype(jnp.bfloat16)


def front(
    tokens,
    attn_gain,
    ffn_gain,
    w_query,
    w_key,
    w_value,
    w_out,
    key_cache,
    value_cache,
    lengths,
    cached,
    pick,
    ids,
    gates,
    replica_owner,
):
    count, width = tokens.shape
    any_space = pl.BlockSpec(memory_space=pl.ANY)
    vmem = pl.BlockSpec(memory_space=pltpu.VMEM)
    smem = pl.BlockSpec(memory_space=pltpu.SMEM)
    dma = pltpu.SemaphoreType.DMA
    bf16 = jnp.bfloat16
    half_dim = HEAD_DIM // 2
    inverse = rope_base ** (-(jnp.arange(half_dim, dtype=jnp.float32) * 2.0 / HEAD_DIM))
    inverse = jnp.concatenate([inverse, inverse])[None, :]
    owners = jnp.pad(replica_owner.T, ((0, 0), (0, 128 - replica_owner.shape[0])))
    return pl.pallas_call(
        front_kernel,
        out_shape=(
            jax.ShapeDtypeStruct((count, width), bf16),
            jax.ShapeDtypeStruct((count, width), bf16),
            jax.ShapeDtypeStruct((8, count), jnp.float32),
            jax.ShapeDtypeStruct((8, 128), jnp.int32),
        ),
        in_specs=[smem] * 3 + [vmem] * 7 + [any_space] * 6,
        out_specs=(vmem,) * 4,
        scratch_shapes=[
            pltpu.VMEM(w_query.shape, bf16),
            pltpu.VMEM(w_key.shape, bf16),
            pltpu.VMEM(w_value.shape, bf16),
            pltpu.VMEM(w_out.shape, bf16),
            pltpu.VMEM((3, KV_HEADS, CACHE, HEAD_DIM), bf16),
            pltpu.VMEM((3, KV_HEADS, CACHE, 2 * HEAD_DIM), bf16),
            pltpu.VMEM((KV_HEADS, count, HEAD_DIM), bf16),
            pltpu.VMEM((KV_HEADS, count, 2 * HEAD_DIM), bf16),
            pltpu.VMEM((HEADS, count, HEAD_DIM), bf16),
            pltpu.VMEM((count, HEADS * HEAD_DIM), bf16),
            dma((4,)),
            dma((3, KV_HEADS)),
            dma((3, KV_HEADS)),
        ],
        name="front",
        compiler_params=pltpu.CompilerParams(vmem_limit_bytes=58 << 20),
    )(
        lengths,
        cached,
        pick,
        tokens,
        attn_gain[None, :],
        ffn_gain[None, :],
        inverse,
        ids,
        gates,
        owners,
        w_query,
        w_key,
        w_value,
        w_out,
        key_cache,
        value_cache,
    )


MESH = pl.DeviceIdType.MESH
SIDE = 4
SLOTS = 32
HALF = 128
WIDTH = 1536
HIDDEN = 768
CHUNK = 2 * SIDE * SLOTS
PARTNERS = [
    (dz, dx, dy, dc)
    for dz in range(SIDE)
    for dx in range(SIDE)
    for dy in range(SIDE)
    for dc in range(2)
    if (dz == 0) + (dx == 0) + (dy == 0) >= 2 and (dz, dx, dy, dc) != (0, 0, 0, 0)
]


def place():
    row, column = lax.axis_index("dp"), lax.axis_index("expert")
    return row // SIDE, row % SIDE, column // 2, column % 2


def device_at(dz, dx, dy, dc):
    z, x, y, c = place()
    row = ((z + dz) % SIDE) * SIDE + (x + dx) % SIDE
    return (row, ((y + dy) % SIDE) * 2 + (c + dc) % 2)


def along(half, offset, dc=0):
    return device_at(half * offset, (1 - half) * offset, 0, dc)


def across(half, offset):
    return device_at((1 - half) * offset, half * offset, 0, 0)


def send(source, landing, sem_s, sem_r, device):
    return pltpu.make_async_remote_copy(
        src_ref=source,
        dst_ref=landing,
        send_sem=sem_s,
        recv_sem=sem_r,
        device_id=device,
        device_id_type=MESH,
    )


def moe_kernel(
    rows_ref,
    table_ref,
    counts_ref,
    residual_ref,
    gate_up_ref,
    down_ref,
    out_ref,
    owner_ref,
    held,
    tables,
    packed,
    landed,
    done,
    back_rows,
    partial,
    given,
    total,
    gate_up,
    down,
    tallies,
    told,
    s_first,
    r_first,
    s_table,
    r_table,
    s_out,
    r_out,
    s_back,
    r_back,
    s_give,
    r_give,
    s_tally,
    r_tally,
    s_weight,
    r_weight,
    s_pass,
    r_pass,
):
    z, x, y, c = place()
    barrier = pltpu.get_barrier_semaphore()
    for offsets in PARTNERS:
        pl.semaphore_signal(barrier, inc=1, device_id=device_at(*offsets), device_id_type=MESH)
    pl.semaphore_wait(barrier, len(PARTNERS))

    first = []
    for half in range(2):
        for back in (1, 3, 2):
            there = across(half, back)
            first.append(
                send(table_ref, tables.at[half, back], s_table.at[half, back], r_table.at[half, back], there)
            )
            first.append(
                send(
                    rows_ref.at[pl.ds(half * HALF, HALF)],
                    held.at[half, back],
                    s_first.at[half, back],
                    r_first.at[half, back],
                    there,
                )
            )
    for copy in first:
        copy.start()

    column = y * 2 + c
    shards = []
    for dc in range(2):
        expert = (c + dc) % 2
        for dy in (1, 3, 0):
            for kind, source, landing in (
                (0, gate_up_ref.at[expert], gate_up.at[:, column]),
                (1, down_ref.at[expert], down.at[column]),
            ):
                if dy == 0 and dc == 0:
                    copy = pltpu.make_async_copy(source, landing, r_weight.at[dy, dc, kind])
                else:
                    copy = send(
                        source,
                        landing,
                        s_weight.at[dy, dc, kind],
                        r_weight.at[dy, dc, kind],
                        device_at(0, 0, dy, dc),
                    )
                copy.start()
                shards.append(copy)

    tallies[0] = counts_ref[...]
    legs = [
        [(0, 1, 0, 0), (0, 2, 0, 0), (0, 3, 0, 0)],
        [(1, 0, 0, 0), (2, 0, 0, 0), (3, 0, 0, 0)],
        [(0, 0, 1, 0), (0, 0, 2, 0), (0, 0, 3, 0)],
        [(0, 0, 0, 1)],
    ]

    def tally(leg):
        copies = [
            send(tallies.at[leg], told.at[leg, k], s_tally.at[leg, k], r_tally.at[leg, k], device_at(*offsets))
            for k, offsets in enumerate(legs[leg])
        ]
        for copy in copies:
            copy.start()
        return copies

    def add_tallies(leg, copies):
        held_so_far = tallies[leg]
        for k, copy in enumerate(copies):
            copy.wait()
            held_so_far = held_so_far + told[leg, k]
        return held_so_far

    telling = tally(0)

    held[0, 0] = rows_ref[0:HALF, :]
    held[1, 0] = rows_ref[HALF : 2 * HALF, :]
    tables[0, 0] = table_ref[...]
    tables[1, 0] = table_ref[...]
    line = lax.broadcasted_iota(jnp.int32, (CHUNK, HALF), 0)

    def copies_out(half, back):
        at = (1 - half) * x + half * z
        copies = []
        for dc in (1, 0):
            for offset in (2, 1, 3, 0):
                piece = packed.at[half, back, (at + offset) % SIDE, (c + dc) % 2]
                landing = landed.at[half, back, offset, dc]
                arrival = r_out.at[half, back, offset, dc]
                if offset == 0 and dc == 0:
                    copies.append(pltpu.make_async_copy(piece, landing, arrival))
                else:
                    copies.append(
                        send(piece, landing, s_out.at[half, back, offset, dc], arrival, along(half, offset, dc))
                    )
        return copies

    def pack(half, back):
        if half == 0:
            wanted = line + z * CHUNK
        else:
            wanted = (line // 64) * CHUNK + x * 64 + line % 64
        table = tables[half, back]
        hot = jnp.zeros((CHUNK, HALF), jnp.bool_)
        for k in range(4):
            code = table[k : k + 1, half * HALF : (half + 1) * HALF].astype(jnp.int32)
            hot = hot | (code == wanted)
        spread = jnp.dot(
            hot.astype(jnp.float32).astype(jnp.bfloat16),
            held[half, back],
            preferred_element_type=jnp.float32,
        ).astype(jnp.bfloat16)
        packed[half, back] = spread.reshape(SIDE, 2, SLOTS, WIDTH)
        for copy in copies_out(half, back):
            copy.start()

    def arrive(half, back):
        send(table_ref, tables.at[half, back], s_table.at[half, back], r_table.at[half, back], across(half, back)).wait_recv()
        send(
            rows_ref.at[pl.ds(half * HALF, HALF)],
            held.at[half, back],
            s_first.at[half, back],
            r_first.at[half, back],
            across(half, back),
        ).wait_recv()

    for half in range(2):
        pack(half, 0)

    def pack_round(step, carry):
        back = 1 + (2 * step) % 3
        for half in range(2):
            arrive(half, back)
            pack(half, back)
        return carry

    lax.fori_loop(0, 3, pack_round, 0)

    passing = []
    for dc in range(2):
        for side, (dy, onward, low) in enumerate(((1, 1, 0), (3, 3, 1))):
            owner = ((y + SIDE - dy) % SIDE) * 2 + (c + dc) % 2
            for kind in range(2):
                if kind == 0:
                    whole, rows = gate_up.at[:, owner], 48
                    piece = gate_up.at[:, owner, pl.ds(low * rows, rows)]
                else:
                    whole, rows = down.at[owner], 96
                    piece = down.at[owner, pl.ds(low * rows, rows)]
                send(whole, whole, s_weight.at[dy, dc, kind], r_weight.at[dy, dc, kind], device_at(0, 0, dy, dc)).wait_recv()
                copy = send(
                    piece, piece, s_pass.at[side, dc, kind], r_pass.at[side, dc, kind], device_at(0, 0, onward, 0)
                )
                copy.start()
                passing.append(copy)

    for leg in range(1, 4):
        tallies[leg] = add_tallies(leg - 1, telling)
        telling = tally(leg)
    tallied = add_tallies(3, telling)
    me = lax.axis_index("dp") * 8 + lax.axis_index("expert")
    lane = lax.broadcasted_iota(jnp.int32, tallied.shape, 1)
    mine = jnp.sum(jnp.where(lane == me, tallied, 0).astype(jnp.float32), axis=1, keepdims=True)
    owner_ref[...] = jnp.broadcast_to(mine, tallied.shape).astype(jnp.int32)

    for kind in range(2):
        for dc in range(2):
            whole = gate_up.at[:, column] if kind == 0 else down.at[column]
            if dc == 0:
                source = gate_up_ref.at[c] if kind == 0 else down_ref.at[c]
                pltpu.make_async_copy(source, whole, r_weight.at[0, 0, kind]).wait()
            else:
                send(
                    whole, whole, s_weight.at[0, dc, kind], r_weight.at[0, dc, kind], device_at(0, 0, 0, 1)
                ).wait_recv()
    for copy in passing:
        copy.wait()

    def copies_back(half, back, own=True):
        copies = []
        for dc in (1, 0):
            for offset in (2, 1, 3, 0):
                if offset == 0 and dc == 0 and not own:
                    continue
                piece = done.at[half, back, offset, dc]
                landing = back_rows.at[half, back, offset, dc]
                arrival = r_back.at[half, back, offset, dc]
                if offset == 0 and dc == 0:
                    copies.append((pltpu.make_async_copy(piece, landing, arrival), False))
                else:
                    copies.append(
                        (
                            send(
                                piece,
                                landing,
                                s_back.at[half, back, offset, dc],
                                arrival,
                                along(half, SIDE - offset, dc),
                            ),
                            True,
                        )
                    )
        return copies

    last = (((1,), (1,)), ((), ()))

    def serve(step, carry):
        half, back = step % 2, (step // 2 + 1) % SIDE
        for copy in copies_out(half, back):
            copy.wait()
        arrived = landed[half, back].reshape(CHUNK, WIDTH)
        gate = lax.dot_general(
            arrived, gate_up[0].reshape(HIDDEN, WIDTH), last, preferred_element_type=jnp.float32
        )
        up = lax.dot_general(
            arrived, gate_up[1].reshape(HIDDEN, WIDTH), last, preferred_element_type=jnp.float32
        )
        hidden = (jnp.maximum(gate, 0.0) * up).astype(jnp.bfloat16)
        answer = lax.dot_general(
            hidden, down[...].reshape(WIDTH, HIDDEN), last, preferred_element_type=jnp.float32
        )
        done[half, back] = answer.astype(jnp.bfloat16).reshape(SIDE, 2, SLOTS, WIDTH)
        for copy, _ in copies_back(half, back):
            copy.start()
        return carry

    lax.fori_loop(0, 2 * SIDE, serve, 0)

    turn, swap, slot = line // 64, (line // 32) % 2, line % 32

    def mix(half, back):
        for copy, remote in copies_back(half, back):
            if remote:
                copy.wait_recv()
            else:
                copy.wait()
        if half == 0:
            owner = z * SIDE + (x + turn) % SIDE
        else:
            owner = ((z + turn) % SIDE) * SIDE + x
        wanted = owner * 64 + ((c + swap) % 2) * 32 + slot
        table = tables[half, back]
        weight = jnp.zeros((CHUNK, HALF), jnp.float32)
        for k in range(4):
            code = table[k : k + 1, half * HALF : (half + 1) * HALF].astype(jnp.int32)
            gate = table[4 + k : 5 + k, half * HALF : (half + 1) * HALF]
            weight = weight + jnp.where(code == wanted, gate, 0.0)
        coarse = weight.astype(jnp.bfloat16)
        fine = (weight - coarse.astype(jnp.float32)).astype(jnp.bfloat16)
        came = back_rows[half, back].reshape(CHUNK, WIDTH)
        rows = (((0,), (0,)), ((), ()))
        return lax.dot_general(
            coarse, came, rows, preferred_element_type=jnp.float32
        ) + lax.dot_general(fine, came, rows, preferred_element_type=jnp.float32)

    def gift(half, back):
        return send(
            partial.at[half, back],
            given.at[half, back],
            s_give.at[half, back],
            r_give.at[half, back],
            across(half, SIDE - back),
        )

    def mix_round(step, carry):
        for half in range(2):
            partial[half, step + 1] = mix(half, step + 1).astype(jnp.bfloat16)
            gift(half, step + 1).start()
        return carry

    lax.fori_loop(0, 3, mix_round, 0)
    for half in range(2):
        total[half] = mix(half, 0)
    for half in range(2):
        mixed = total[half]
        for back in (1, 2, 3):
            gift(half, back).wait_recv()
            mixed = mixed + given[half, back].astype(jnp.float32)
        here = pl.ds(half * HALF, HALF)
        out_ref[here, :] = (residual_ref[here, :].astype(jnp.float32) + mixed).astype(jnp.bfloat16)

    for copy in first:
        copy.wait_send()
    position = 0
    for dc in range(2):
        for dy in (1, 3, 0):
            for kind in range(2):
                if not (dy == 0 and dc == 0):
                    shards[position].wait_send()
                position += 1

    def settle(step, carry):
        half, back = step % 2, step // 2
        for copy, _ in copies_back(half, back, own=False):
            copy.wait_send()
        return carry

    lax.fori_loop(0, 2 * SIDE, settle, 0)
    for half in range(2):
        for back in (1, 2, 3):
            gift(half, back).wait_send()


def moe(rows, table, counts, residual, gate_up, down):
    any_space = pl.BlockSpec(memory_space=pl.ANY)
    vmem = pl.BlockSpec(memory_space=pltpu.VMEM)
    dma = pltpu.SemaphoreType.DMA
    chunks = (2, SIDE, SIDE, 2, SLOTS, WIDTH)
    halves = (2, SIDE, HALF, WIDTH)
    bf16 = jnp.bfloat16
    return pl.pallas_call(
        moe_kernel,
        out_shape=(
            jax.ShapeDtypeStruct((2 * HALF, WIDTH), bf16),
            jax.ShapeDtypeStruct((8, 128), jnp.int32),
        ),
        in_specs=[vmem, vmem, vmem, vmem, any_space, any_space],
        out_specs=(vmem, vmem),
        scratch_shapes=[
            pltpu.VMEM(halves, bf16),
            pltpu.VMEM((2, SIDE, 8, 2 * HALF), jnp.float32),
            pltpu.VMEM(chunks, bf16),
            pltpu.VMEM(chunks, bf16),
            pltpu.VMEM(chunks, bf16),
            pltpu.VMEM(chunks, bf16),
            pltpu.VMEM(halves, bf16),
            pltpu.VMEM(halves, bf16),
            pltpu.VMEM((2, HALF, WIDTH), jnp.float32),
            pltpu.VMEM((2, 8, 96, WIDTH), bf16),
            pltpu.VMEM((8, 192, HIDDEN), bf16),
            pltpu.VMEM((4, 8, 128), jnp.int32),
            pltpu.VMEM((4, 3, 8, 128), jnp.int32),
            dma((2, SIDE)),
            dma((2, SIDE)),
            dma((2, SIDE)),
            dma((2, SIDE)),
            dma((2, SIDE, SIDE, 2)),
            dma((2, SIDE, SIDE, 2)),
            dma((2, SIDE, SIDE, 2)),
            dma((2, SIDE, SIDE, 2)),
            dma((2, SIDE)),
            dma((2, SIDE)),
            dma((4, 3)),
            dma((4, 3)),
            dma((SIDE, 2, 2)),
            dma((SIDE, 2, 2)),
            dma((2, 2, 2)),
            dma((2, 2, 2)),
        ],
        name="moe",
        compiler_params=pltpu.CompilerParams(
            collective_id=1, has_side_effects=True, vmem_limit_bytes=60 << 20
        ),
        cost_estimate=pl.CostEstimate(flops=17 * 10**9, bytes_accessed=10**7, transcendentals=0),
    )(rows, table, counts, residual, gate_up, down)


def on_device(
    tokens,
    attn_gain,
    ffn_gain,
    w_query,
    w_key,
    w_value,
    w_out,
    key_cache,
    value_cache,
    req_lengths,
    cache_lengths,
    expert_ids,
    route_gate,
    replica_owner,
    replica_pick,
    w_gate_up,
    w_down,
):
    residual, normed_mid, table, counts = front(
        tokens,
        attn_gain,
        ffn_gain,
        w_query,
        w_key,
        w_value,
        w_out,
        key_cache,
        value_cache,
        req_lengths,
        cache_lengths,
        replica_pick,
        expert_ids,
        route_gate,
        replica_owner,
    )
    layer_out, owner_counts = moe(
        normed_mid, table, counts, residual, w_gate_up.transpose(0, 2, 1, 3), w_down
    )
    return (layer_out, owner_counts[: w_gate_up.shape[0], 0][None, :])


def solution(mesh):
    in_specs = (
        P(("dp", "expert"), None),
        P(),
        P(),
        P(),
        P(),
        P(),
        P(),
        P(("dp", "expert"), None, None),
        P(("dp", "expert"), None, None),
        P(("dp", "expert"), None),
        P(("dp", "expert"), None),
        P(("dp", "expert"), None),
        P(("dp", "expert"), None),
        P(),
        P(("dp", "expert"), None),
        P("dp", "expert", None, None),
        P("dp", "expert", None),
    )
    out_specs = (P(("dp", "expert"), None), P(("dp", "expert"), None))
    return jax.shard_map(
        on_device, mesh=mesh, in_specs=in_specs, out_specs=out_specs, check_vma=False
    )
```

profile of v0, /device:TPU:1, one launch (start us, length us, event | category | flops | bytes accessed | tf_op | source)
XLA Modules:
  0.0 176.4 jit_solution(2133111960304139615)
XLA Ops:
  0.6 0.6 maximum_bitcast_fusion.inverse_ref
  1.2 1.3 pad.4.owners_ref
  2.5 1.3 broadcast_in_dim.9.attn_gain_ref
  3.8 1.3 broadcast_in_dim.10.ffn_gain_ref
  5.1 1.5 copy.22.ids_ref
  6.6 1.5 copy.23.gate_ref
  8.1 2.4 %copy.26 = bf16[2,96,2,1536]{3,1,2,0:T(8,128)(2,1)} copy(bf16[2,96,2,1536]{3,2,1,0:T(2,128)(2,1)} %param.32) | data formatting | bytes 2359296 | tf_op args[15]
  10.5 28.1 %front.1 = (bf16[256,1536]{1,0:T(8,128)(2,1)}, bf16[256,1536]{1,0:T(8,128)(2,1)}, f32[8,256]{1,0:T(8,128)}, s32[8,128]{1,0:T(8,128)}) custom-call(s32[1,3]{1,0:T(1,128)} %lengths_ref.1, s32[1,3]{1,0:T(1,128)} %cached_ref.1, s32[1,8]{1,0:T(1,128)} %pick_ref.1, bf16[256,1536]{1,0:T(8,128)(2,1)} %tokens_ref.1, f32[1,1536]{1,0:T(1,128)} %broadcast_in_dim.9.attn_gain_ref, ...), custom_call_target="tpu_custom_call" | custom-call | tf_op jit(solution)/shard_map/front/pallas_call | solution.py:282
  38.6 134.4 %moe.1 = (bf16[256,1536]{1,0:T(8,128)(2,1)}, s32[8,128]{1,0:T(8,128)}) custom-call(bf16[256,1536]{1,0:T(8,128)(2,1)} %get-tuple-element.8.rows_ref, f32[8,256]{1,0:T(8,128)} %get-tuple-element.9.table_ref, s32[8,128]{1,0:T(8,128)} %get-tuple-element.10.counts_ref, bf16[256,1536]{1,0:T(8,128)(2,1)} %get-tuple-element.11.residual_ref, ...), custom_call_target="tpu_custom_call" | custom-call | flops 16999999488 | bytes 10000000 | tf_op jit(solution)/shard_map/moe/pallas_call | solution.py:723
  173.0 1.3 slice_reduce_fusion
  174.3 2.1 %copy.28 = bf16[256,1536]{1,0:T(8,128)(2,1)} copy(bf16[256,1536]{1,0:T(8,128)(2,1)} %get-tuple-element.16) | data formatting | bytes 1572864
  (1 shorter events, 0.0 us)
where the time goes:
time: 177 us; the launch traced here: 176 us
  Pallas kernels  163 us (92%)
  local copies, waits for them, and re-layouts  12.6 us (7%)
    pallas_call x1, Pallas kernels, moe(): pl.pallas_call(moe_kernel, out_shape=(jax.ShapeDtypeStruct((2 * HALF, WID...  134 us
    pallas_call x1, Pallas kernels, front(): pl.pallas_call(front_kernel, out_shape=(jax.ShapeDtypeStruct((count, widt...  28.1 us
    unnamed x4, local copies, waits for them, and re-layouts  7.43 us

commit v1 on v0

--- a/solution.py
+++ b/solution.py
@@ -1,5 +1,6 @@
 import jax
 import jax.numpy as jnp
+import numpy as np
 from jax import lax
 from jax.experimental import pallas as pl
 from jax.experimental.pallas import tpu as pltpu
@@ -99,38 +100,44 @@
 
     lane = lax.broadcasted_iota(jnp.int32, (count, 128), 1)
     row = lax.broadcasted_iota(jnp.int32, (count, 128), 0)
-    hots = [(ids_ref[:, k : k + 1] == lane).astype(jnp.float32) for k in range(4)]
-    hot = hots[0] + hots[1] + hots[2] + hots[3]
-    later = lax.broadcasted_iota(jnp.int32, (count, count), 0)
-    sooner = lax.broadcasted_iota(jnp.int32, (count, count), 1)
+    expert = lax.broadcasted_iota(jnp.int32, (32, count), 0)
+    ids = [ids_ref[k : k + 1, :] for k in range(4)]
+    hots = [(ids[k] == expert).astype(jnp.float32) for k in range(4)]
+    hot = (hots[0] + hots[1] + hots[2] + hots[3]).astype(jnp.bfloat16)
+    sooner = lax.broadcasted_iota(jnp.int32, (count, count), 0)
+    later = lax.broadcasted_iota(jnp.int32, (count, count), 1)
     before = jnp.dot(
+        hot,
         ((later // 32 == sooner // 32) & (sooner < later)).astype(jnp.float32).astype(jnp.bfloat16),
-        hot.astype(jnp.bfloat16),
         preferred_element_type=jnp.float32,
     )
-    columns = jnp.zeros((count, 128), jnp.float32)
+    line = lax.broadcasted_iota(jnp.int32, (8, count), 0)
+    offset = lax.broadcasted_iota(jnp.int32, (1, count), 1) // 32 % 4 * 8
+    table = jnp.zeros((8, count), jnp.float32)
     for k in range(4):
-        rank = jnp.sum(hots[k] * before, axis=1, keepdims=True)
-        code = (ids_ref[:, k : k + 1] * 32).astype(jnp.float32) + rank
-        columns = jnp.where(lane == k, code, columns)
-        columns = jnp.where(lane == 4 + k, gate_ref[:, k : k + 1], columns)
-    columns = columns + jnp.where(lane < 4, ((row // 32) % 4 * 8).astype(jnp.float32), 0.0)
-    table_ref[...] = columns.T[0:8, :]
-
-    blocks = lax.broadcasted_iota(jnp.int32, (8, count), 0)
+        rank = jnp.sum(hots[k] * before, axis=0, keepdims=True)
+        code = (ids[k] * 32 + offset).astype(jnp.float32) + rank
+        table = jnp.where(line == k, code, table)
+        table = jnp.where(line == 4 + k, gate_ref[k : k + 1, :], table)
+    table_ref[...] = table
+
     members = lax.broadcasted_iota(jnp.int32, (8, count), 1)
-    per_block = jnp.dot(
-        (members // 32 == blocks).astype(jnp.float32).astype(jnp.bfloat16),
-        hot.astype(jnp.bfloat16),
+    last = (((1,), (1,)), ((), ()))
+    per_block = lax.dot_general(
+        (members // 32 == line).astype(jnp.float32).astype(jnp.bfloat16),
+        hot,
+        last,
         preferred_element_type=jnp.float32,
     )
-    place_of = lax.broadcasted_iota(jnp.int32, (8, 128), 0)
-    per_owner = jnp.zeros((8, 128), jnp.float32)
+    place_of = lax.broadcasted_iota(jnp.int32, (8, 32), 0)
+    per_owner = jnp.zeros((8, 32), jnp.float32)
     for block in range(8):
         owner = owners_ref[pl.ds(pick_ref[0, block], 1), :]
         per_owner = per_owner + jnp.where(place_of == owner, per_block[block : block + 1, :], 0.0)
-    expert_row = lax.broadcasted_iota(jnp.int32, (128, 128), 0)
-    owner_lane = lax.broadcasted_iota(jnp.int32, (128, 128), 1)
+    expert_row = lax.broadcasted_iota(jnp.int32, (32, 128), 0)
+    owner_lane = lax.broadcasted_iota(jnp.int32, (32, 128), 1)
+    own_line = lax.broadcasted_iota(jnp.int32, (8, 128), 0)
+    own_lane = lax.broadcasted_iota(jnp.int32, (8, 128), 1)
     tallied = jnp.zeros((8, 128), jnp.float32)
     for j in range(2):
         moved = jnp.dot(
@@ -138,12 +145,8 @@
             (expert_row == owner_lane // 8 * 2 + j).astype(jnp.float32).astype(jnp.bfloat16),
             preferred_element_type=jnp.float32,
         )
-        own = jnp.sum(
-            jnp.where(lax.broadcasted_iota(jnp.int32, (8, 128), 1) % 8 == place_of, moved, 0.0),
-            axis=0,
-            keepdims=True,
-        )
-        tallied = jnp.where(place_of == j, own, tallied)
+        own = jnp.sum(jnp.where(own_lane % 8 == own_line, moved, 0.0), axis=0, keepdims=True)
+        tallied = jnp.where(own_line == j, own, tallied)
     counts_ref[...] = tallied.astype(jnp.int32)
 
     for request in range(3):
@@ -154,7 +157,7 @@
 
     wide = tokens_ref[...].astype(jnp.float32)
     scale = lax.rsqrt(jnp.mean(wide * wide, axis=1, keepdims=True) + epsilon)
-    normed = (wide * scale * attn_gain_ref[...]).astype(jnp.bfloat16)
+    normed = (wide * scale * attn_gain_ref[...].reshape(1, -1)).astype(jnp.bfloat16)
 
     position = row + by_request(row, [cached[0], cached[1] - starts[1], cached[2] - starts[2]])
     angle = position.astype(jnp.float32) * inverse_ref[...]
@@ -185,7 +188,6 @@
 
     factor = HEAD_DIM ** (-0.5) * 1.4426950408889634
     stack = GROUP * TILE
-    last = (((1,), (1,)), ((), ()))
     lowest = -jnp.inf
     for request in range(3):
         for copy in cache_loads(request):
@@ -249,7 +251,7 @@
     residual_ref[...] = residual
     wide = residual.astype(jnp.float32)
     scale = lax.rsqrt(jnp.mean(wide * wide, axis=1, keepdims=True) + epsilon)
-    normed_ref[...] = (wide * scale * ffn_gain_ref[...]).astype(jnp.bfloat16)
+    normed_ref[...] = (wide * scale * ffn_gain_ref[...].reshape(1, -1)).astype(jnp.bfloat16)
 
 
 def front(
@@ -275,10 +277,8 @@
     smem = pl.BlockSpec(memory_space=pltpu.SMEM)
     dma = pltpu.SemaphoreType.DMA
     bf16 = jnp.bfloat16
-    half_dim = HEAD_DIM // 2
-    inverse = rope_base ** (-(jnp.arange(half_dim, dtype=jnp.float32) * 2.0 / HEAD_DIM))
-    inverse = jnp.concatenate([inverse, inverse])[None, :]
-    owners = jnp.pad(replica_owner.T, ((0, 0), (0, 128 - replica_owner.shape[0])))
+    rates = np.float32(rope_base) ** (-(np.arange(HEAD_DIM // 2, dtype=np.float32) * 2.0 / HEAD_DIM))
+    inverse = jnp.asarray(np.concatenate([rates, rates])[None, :].astype(np.float32))
     return pl.pallas_call(
         front_kernel,
         out_shape=(
@@ -306,17 +306,18 @@
         ],
         name="front",
         compiler_params=pltpu.CompilerParams(vmem_limit_bytes=58 << 20),
+        cost_estimate=pl.CostEstimate(flops=12 * 10**9, bytes_accessed=60 * 10**6, transcendentals=10**7),
     )(
         lengths,
         cached,
         pick,
         tokens,
-        attn_gain[None, :],
-        ffn_gain[None, :],
+        attn_gain,
+        ffn_gain,
         inverse,
-        ids,
-        gates,
-        owners,
+        ids.T,
+        gates.T,
+        replica_owner.T,
         w_query,
         w_key,
         w_value,
@@ -411,6 +412,12 @@
     r_weight,
     s_pass,
     r_pass,
+    d_down,
+    s_relay,
+    r_relay,
+    lent,
+    s_lend,
+    r_lend,
 ):
     z, x, y, c = place()
     barrier = pltpu.get_barrier_semaphore()
@@ -419,45 +426,41 @@
     pl.semaphore_wait(barrier, len(PARTNERS))
 
     first = []
-    for half in range(2):
-        for back in (1, 3, 2):
+    for back in (1, 3, 2):
+        for half in range(2):
             there = across(half, back)
             first.append(
                 send(table_ref, tables.at[half, back], s_table.at[half, back], r_table.at[half, back], there)
             )
-            first.append(
-                send(
-                    rows_ref.at[pl.ds(half * HALF, HALF)],
-                    held.at[half, back],
-                    s_first.at[half, back],
-                    r_first.at[half, back],
-                    there,
+            if back != 2:
+                first.append(
+                    send(
+                        rows_ref.at[pl.ds(half * HALF, HALF)],
+                        held.at[half, back],
+                        s_first.at[half, back],
+                        r_first.at[half, back],
+                        there,
+                    )
                 )
-            )
     for copy in first:
         copy.start()
 
     column = y * 2 + c
-    shards = []
+    shards = {}
     for dc in range(2):
         expert = (c + dc) % 2
         for dy in (1, 3, 0):
-            for kind, source, landing in (
-                (0, gate_up_ref.at[expert], gate_up.at[:, column]),
-                (1, down_ref.at[expert], down.at[column]),
-            ):
-                if dy == 0 and dc == 0:
-                    copy = pltpu.make_async_copy(source, landing, r_weight.at[dy, dc, kind])
-                else:
-                    copy = send(
-                        source,
-                        landing,
-                        s_weight.at[dy, dc, kind],
-                        r_weight.at[dy, dc, kind],
-                        device_at(0, 0, dy, dc),
-                    )
-                copy.start()
-                shards.append(copy)
+            source, landing = gate_up_ref.at[expert], gate_up.at[:, column]
+            if dy == 0 and dc == 0:
+                own_shard = pltpu.make_async_copy(source, landing, r_weight.at[dy, dc])
+                own_shard.start()
+            else:
+                shards[dy, dc] = send(
+                    source, landing, s_weight.at[dy, dc], r_weight.at[dy, dc], device_at(0, 0, dy, dc)
+                )
+                shards[dy, dc].start()
+    own_down = pltpu.make_async_copy(down_ref.at[c], down, d_down)
+    own_down.start()
 
     tallies[0] = counts_ref[...]
     legs = [
@@ -526,65 +529,64 @@
         for copy in copies_out(half, back):
             copy.start()
 
+    def relay(half, side):
+        rows = pl.ds(side * (HALF // 2), HALF // 2)
+        return send(
+            held.at[half, 1 + 2 * side, rows],
+            held.at[half, 2, rows],
+            s_relay.at[half, side],
+            r_relay.at[half, side],
+            across(half, 1 + 2 * side),
+        )
+
     def arrive(half, back):
-        send(table_ref, tables.at[half, back], s_table.at[half, back], r_table.at[half, back], across(half, back)).wait_recv()
         send(
-            rows_ref.at[pl.ds(half * HALF, HALF)],
-            held.at[half, back],
-            s_first.at[half, back],
-            r_first.at[half, back],
+            table_ref,
+            tables.at[half, back],
+            s_table.at[half, back],
+            r_table.at[half, back],
             across(half, back),
         ).wait_recv()
+        if back == 2:
+            for side in range(2):
+                relay(half, side).wait_recv()
+        else:
+            send(
+                rows_ref.at[pl.ds(half * HALF, HALF)],
+                held.at[half, back],
+                s_first.at[half, back],
+                r_first.at[half, back],
+                across(half, back),
+            ).wait_recv()
+            relay(half, back // 2).start()
 
     for half in range(2):
         pack(half, 0)
-
-    def pack_round(step, carry):
-        back = 1 + (2 * step) % 3
+    for back in (1, 3, 2):
         for half in range(2):
             arrive(half, back)
+        for half in range(2):
             pack(half, back)
-        return carry
-
-    lax.fori_loop(0, 3, pack_round, 0)
 
     passing = []
     for dc in range(2):
         for side, (dy, onward, low) in enumerate(((1, 1, 0), (3, 3, 1))):
             owner = ((y + SIDE - dy) % SIDE) * 2 + (c + dc) % 2
-            for kind in range(2):
-                if kind == 0:
-                    whole, rows = gate_up.at[:, owner], 48
-                    piece = gate_up.at[:, owner, pl.ds(low * rows, rows)]
-                else:
-                    whole, rows = down.at[owner], 96
-                    piece = down.at[owner, pl.ds(low * rows, rows)]
-                send(whole, whole, s_weight.at[dy, dc, kind], r_weight.at[dy, dc, kind], device_at(0, 0, dy, dc)).wait_recv()
-                copy = send(
-                    piece, piece, s_pass.at[side, dc, kind], r_pass.at[side, dc, kind], device_at(0, 0, onward, 0)
-                )
-                copy.start()
-                passing.append(copy)
-
-    for leg in range(1, 4):
-        tallies[leg] = add_tallies(leg - 1, telling)
-        telling = tally(leg)
-    tallied = add_tallies(3, telling)
-    me = lax.axis_index("dp") * 8 + lax.axis_index("expert")
-    lane = lax.broadcasted_iota(jnp.int32, tallied.shape, 1)
-    mine = jnp.sum(jnp.where(lane == me, tallied, 0).astype(jnp.float32), axis=1, keepdims=True)
-    owner_ref[...] = jnp.broadcast_to(mine, tallied.shape).astype(jnp.int32)
-
-    for kind in range(2):
-        for dc in range(2):
-            whole = gate_up.at[:, column] if kind == 0 else down.at[column]
-            if dc == 0:
-                source = gate_up_ref.at[c] if kind == 0 else down_ref.at[c]
-                pltpu.make_async_copy(source, whole, r_weight.at[0, 0, kind]).wait()
-            else:
-                send(
-                    whole, whole, s_weight.at[0, dc, kind], r_weight.at[0, dc, kind], device_at(0, 0, 0, 1)
-                ).wait_recv()
+            whole = gate_up.at[:, owner]
+            piece = gate_up.at[:, owner, pl.ds(low * 48, 48)]
+            send(whole, whole, s_weight.at[dy, dc], r_weight.at[dy, dc], device_at(0, 0, dy, dc)).wait_recv()
+            copy = send(
+                piece, piece, s_pass.at[side, dc], r_pass.at[side, dc], device_at(0, 0, onward, 0)
+            )
+            copy.start()
+            passing.append(copy)
+
+    tallies[1] = add_tallies(0, telling)
+    telling = tally(1)
+
+    own_down.wait()
+    own_shard.wait()
+    shards[0, 1].wait_recv()
     for copy in passing:
         copy.wait()
 
@@ -617,7 +619,8 @@
     last = (((1,), (1,)), ((), ()))
 
     def serve(step, carry):
-        half, back = step % 2, (step // 2 + 1) % SIDE
+        turn_at = step // 2
+        half, back = step % 2, 2 - turn_at + 3 * (turn_at // 2) - 2 * (turn_at // 3)
         for copy in copies_out(half, back):
             copy.wait()
         arrived = landed[half, back].reshape(CHUNK, WIDTH)
@@ -629,7 +632,7 @@
         )
         hidden = (jnp.maximum(gate, 0.0) * up).astype(jnp.bfloat16)
         answer = lax.dot_general(
-            hidden, down[...].reshape(WIDTH, HIDDEN), last, preferred_element_type=jnp.float32
+            hidden, down[...], last, preferred_element_type=jnp.float32
         )
         done[half, back] = answer.astype(jnp.bfloat16).reshape(SIDE, 2, SLOTS, WIDTH)
         for copy, _ in copies_back(half, back):
@@ -637,6 +640,8 @@
         return carry
 
     lax.fori_loop(0, 2 * SIDE, serve, 0)
+    tallies[2] = add_tallies(1, telling)
+    telling = tally(2)
 
     turn, swap, slot = line // 64, (line // 32) % 2, line % 32
 
@@ -674,18 +679,42 @@
             across(half, SIDE - back),
         )
 
-    def mix_round(step, carry):
+    def lend(half, side):
+        rows = pl.ds(side * (HALF // 2), HALF // 2)
+        return send(
+            partial.at[half, 2, rows],
+            lent.at[half, side],
+            s_lend.at[half, side],
+            r_lend.at[half, side],
+            across(half, 3 - 2 * side),
+        )
+
+    for half in range(2):
+        partial[half, 2] = mix(half, 2).astype(jnp.bfloat16)
+        for side in range(2):
+            lend(half, side).start()
+    for side in range(2):
+        back = 1 + 2 * side
         for half in range(2):
-            partial[half, step + 1] = mix(half, step + 1).astype(jnp.bfloat16)
-            gift(half, step + 1).start()
-        return carry
-
-    lax.fori_loop(0, 3, mix_round, 0)
+            share = mix(half, back)
+            lend(half, side).wait_recv()
+            rows = slice(side * (HALF // 2), (side + 1) * (HALF // 2))
+            others = slice((1 - side) * (HALF // 2), (2 - side) * (HALF // 2))
+            partial[half, back, rows] = (share[rows] + lent[half, side].astype(jnp.float32)).astype(jnp.bfloat16)
+            partial[half, back, others] = share[others].astype(jnp.bfloat16)
+            gift(half, back).start()
+    tallies[3] = add_tallies(2, telling)
+    telling = tally(3)
     for half in range(2):
         total[half] = mix(half, 0)
+    tallied = add_tallies(3, telling)
+    me = lax.axis_index("dp") * 8 + lax.axis_index("expert")
+    lane = lax.broadcasted_iota(jnp.int32, tallied.shape, 1)
+    mine = jnp.sum(jnp.where(lane == me, tallied, 0).astype(jnp.float32), axis=1, keepdims=True)
+    owner_ref[...] = jnp.broadcast_to(mine, tallied.shape).astype(jnp.int32)
     for half in range(2):
         mixed = total[half]
-        for back in (1, 2, 3):
+        for back in (1, 3):
             gift(half, back).wait_recv()
             mixed = mixed + given[half, back].astype(jnp.float32)
         here = pl.ds(half * HALF, HALF)
@@ -693,13 +722,11 @@
 
     for copy in first:
         copy.wait_send()
-    position = 0
-    for dc in range(2):
-        for dy in (1, 3, 0):
-            for kind in range(2):
-                if not (dy == 0 and dc == 0):
-                    shards[position].wait_send()
-                position += 1
+    for half in range(2):
+        for side in range(2):
+            relay(half, side).wait_send()
+    for copy in shards.values():
+        copy.wait_send()
 
     def settle(step, carry):
         half, back = step % 2, step // 2
@@ -709,8 +736,10 @@
 
     lax.fori_loop(0, 2 * SIDE, settle, 0)
     for half in range(2):
-        for back in (1, 2, 3):
+        for back in (1, 3):
             gift(half, back).wait_send()
+        for side in range(2):
+            lend(half, side).wait_send()
 
 
 def moe(rows, table, counts, residual, gate_up, down):
@@ -739,7 +768,7 @@
             pltpu.VMEM(halves, bf16),
             pltpu.VMEM((2, HALF, WIDTH), jnp.float32),
             pltpu.VMEM((2, 8, 96, WIDTH), bf16),
-            pltpu.VMEM((8, 192, HIDDEN), bf16),
+            pltpu.VMEM((WIDTH, HIDDEN), bf16),
             pltpu.VMEM((4, 8, 128), jnp.int32),
             pltpu.VMEM((4, 3, 8, 128), jnp.int32),
             dma((2, SIDE)),
@@ -754,10 +783,16 @@
             dma((2, SIDE)),
             dma((4, 3)),
             dma((4, 3)),
-            dma((SIDE, 2, 2)),
-            dma((SIDE, 2, 2)),
-            dma((2, 2, 2)),
-            dma((2, 2, 2)),
+            dma((SIDE, 2)),
+            dma((SIDE, 2)),
+            dma((2, 2)),
+            dma((2, 2)),
+            dma(()),
+            dma((2, 2)),
+            dma((2, 2)),
+            pltpu.VMEM((2, 2, HALF // 2, WIDTH), bf16),
+            dma((2, 2)),
+            dma((2, 2)),
         ],
         name="moe",
         compiler_params=pltpu.CompilerParams(
@@ -786,6 +821,7 @@
     w_gate_up,
     w_down,
 ):
+    down = lax.all_gather(w_down, "expert", axis=1, tiled=True)
     residual, normed_mid, table, counts = front(
         tokens,
         attn_gain,
@@ -804,7 +840,7 @@
         replica_owner,
     )
     layer_out, owner_counts = moe(
-        normed_mid, table, counts, residual, w_gate_up.transpose(0, 2, 1, 3), w_down
+        normed_mid, table, counts, residual, w_gate_up.transpose(0, 2, 1, 3), down
     )
     return (layer_out, owner_counts[: w_gate_up.shape[0], 0][None, :])
 

time: 177 us -> 173 us (0.977)
  Pallas kernels: 163 us -> 143 us
  between operations: 0.65 us -> 14 us
  waiting for transfers between devices: 0 us -> 10.5 us
  local copies, waits for them, and re-layouts: 12.6 us -> 5.82 us
    pallas_call x1, Pallas kernels: 134 us -> 115 us  [moe(): pl.pallas_call(moe_kernel, out_shape=(jax.ShapeDtypeStruct((2 * HALF, WID...]
    all_gather x0 -> x1, waiting for transfers between devices: none -> 9.78 us  [on_device(): down = lax.all_gather(w_down, 'expert', axis=1, tiled=True)]
    unnamed x4 -> x2, local copies, waits for them, and re-layouts: 7.43 us -> 4.52 us
    broadcast_in_dim x2 -> x0, local copies, waits for them, and re-layouts: 2.59 us -> none  [the longest x1 1.29 us: front(): ffn_gain[None, :]]
  transfers between devices with their start and end apart: 0 -> 1, of which waited for: 0 -> 1; matrix products, arithmetic and copies ran while one was open for 0% -> 1% of each run, Pallas kernels for 0% -> 16%
where the time goes in v1:
time: 173 us
  Pallas kernels  143 us (83%)
  between operations  14 us (8%)
  waiting for transfers between devices  10.5 us (6%)
  local copies, waits for them, and re-layouts  5.82 us (3%)
    pallas_call x1, Pallas kernels, moe(): pl.pallas_call(moe_kernel, out_shape=(jax.ShapeDtypeStruct((2 * HALF, WID...  115 us
    pallas_call x1, Pallas kernels, front(): pl.pallas_call(front_kernel, out_shape=(jax.ShapeDtypeStruct((count, widt...  27.5 us
    all_gather x1, waiting for transfers between devices, on_device(): down = lax.all_gather(w_down, 'expert', axis=1, tiled=True)  9.78 us
    unnamed x2, local copies, waits for them, and re-layouts  4.52 us
  transfers between devices with their start and end apart: 1, of which 1 were waited for; matrix products, arithmetic and copies ran while one was open for 1% of the time, Pallas kernels for 16%

profile of v1, /device:TPU:1, one launch (start us, length us, event | category | flops | bytes accessed | tf_op | source)
XLA Modules:
  0.0 173.1 jit_solution(13005291025026941388)
XLA Ops:
  7.2 0.0 all-gather.2.cloned.1.call-start
  7.2 0.7 all-gather.2.cloned.1.call-update
  7.9 2.5 %copy.23 = bf16[2,96,2,1536]{3,1,2,0:T(8,128)(2,1)} copy(bf16[2,96,2,1536]{3,2,1,0:T(2,128)(2,1)} %param.33) | data formatting | bytes 2359296 | tf_op args[15]
  10.4 27.5 %front.1 = (bf16[256,1536]{1,0:T(8,128)(2,1)}, bf16[256,1536]{1,0:T(8,128)(2,1)}, f32[8,256]{1,0:T(8,128)}, s32[8,128]{1,0:T(8,128)}) custom-call(s32[1,3]{1,0:T(1,128)} %lengths_ref.1, s32[1,3]{1,0:T(1,128)} %cached_ref.1, s32[1,8]{1,0:T(1,128)} %pick_ref.1, bf16[256,1536]{1,0:T(8,128)(2,1)} %tokens_ref.1, f32[1536]{0:T(1024)} %attn_gain_ref.1, ...), custom_call_target="tpu_custom_call" | custom-call | flops 12000000000 | bytes 60000000 | tf_op jit(solution)/shard_map/front/pallas_call | solution.py:282
  37.9 9.8 %all-gather.2.cloned.1.call-done.down_ref = bf16[2,1536,768]{2,1,0:T(8,128)(2,1)} async-done(((bf16[2,192,768]{2,1,0:T(8,128)(2,1)}), bf16[2,1536,768]{2,1,0:T(8,128)(2,1)}) %all-gather.2.cloned.1.call-update) | async-done | bytes 4718608 | tf_op jit(solution)/shard_map/all_gather | solution.py:824
  47.7 115.2 %moe.1 = (bf16[256,1536]{1,0:T(8,128)(2,1)}, s32[8,128]{1,0:T(8,128)}) custom-call(bf16[256,1536]{1,0:T(8,128)(2,1)} %get-tuple-element.8.rows_ref, f32[8,256]{1,0:T(8,128)} %get-tuple-element.9.table_ref, s32[8,128]{1,0:T(8,128)} %get-tuple-element.10.counts_ref, bf16[256,1536]{1,0:T(8,128)(2,1)} %get-tuple-element.11.residual_ref, ...), custom_call_target="tpu_custom_call" | custom-call | flops 16999999488 | bytes 10000000 | tf_op jit(solution)/shard_map/moe/pallas_call | solution.py:752
  162.9 1.3 slice_reduce_fusion
  164.2 2.1 %copy.25 = bf16[256,1536]{1,0:T(8,128)(2,1)} copy(bf16[256,1536]{1,0:T(8,128)(2,1)} %get-tuple-element.16) | data formatting | bytes 1572864
Async XLA Ops:
  7.2 40.5 %all-gather.2.cloned.1.call-start = ((), (), s32[]{:S(2)}) async-start(), calls=%async_computation | async-start | bytes 5308416 | tf_op jit(solution)/shard_map/all_gather | solution.py:824
Sparse Core Ops, SparseCore 0:
  9.7 37.9 all-gather.1

commit v2 on v1

--- a/solution.py
+++ b/solution.py
@@ -380,7 +380,10 @@
     counts_ref,
     residual_ref,
     gate_up_ref,
-    down_ref,
+    down_a,
+    down_b,
+    down_c,
+    down_d,
     out_ref,
     owner_ref,
     held,
@@ -413,12 +416,15 @@
     s_pass,
     r_pass,
     d_down,
+    s_down,
+    r_down,
     s_relay,
     r_relay,
     lent,
     s_lend,
     r_lend,
 ):
+    down_refs = (down_a, down_b, down_c, down_d)
     z, x, y, c = place()
     barrier = pltpu.get_barrier_semaphore()
     for offsets in PARTNERS:
@@ -459,8 +465,15 @@
                     source, landing, s_weight.at[dy, dc], r_weight.at[dy, dc], device_at(0, 0, dy, dc)
                 )
                 shards[dy, dc].start()
-    own_down = pltpu.make_async_copy(down_ref.at[c], down, d_down)
-    own_down.start()
+    near_down, far_down = [], []
+    for back, shard in enumerate(down_refs):
+        spot = down.at[((y + SIDE - back) % SIDE) * 2 + c]
+        near_down.append(pltpu.make_async_copy(shard.at[c], spot, d_down.at[back]))
+        far_down.append(
+            send(shard.at[1 - c], spot, s_down.at[back], r_down.at[back], device_at(0, 0, 0, 1))
+        )
+    for copy in near_down + far_down:
+        copy.start()
 
     tallies[0] = counts_ref[...]
     legs = [
@@ -584,7 +597,10 @@
     tallies[1] = add_tallies(0, telling)
     telling = tally(1)
 
-    own_down.wait()
+    for copy in near_down:
+        copy.wait()
+    for copy in far_down:
+        copy.wait_recv()
     own_shard.wait()
     shards[0, 1].wait_recv()
     for copy in passing:
@@ -632,7 +648,7 @@
         )
         hidden = (jnp.maximum(gate, 0.0) * up).astype(jnp.bfloat16)
         answer = lax.dot_general(
-            hidden, down[...], last, preferred_element_type=jnp.float32
+            hidden, down[...].reshape(WIDTH, HIDDEN), last, preferred_element_type=jnp.float32
         )
         done[half, back] = answer.astype(jnp.bfloat16).reshape(SIDE, 2, SLOTS, WIDTH)
         for copy, _ in copies_back(half, back):
@@ -711,7 +727,9 @@
     me = lax.axis_index("dp") * 8 + lax.axis_index("expert")
     lane = lax.broadcasted_iota(jnp.int32, tallied.shape, 1)
     mine = jnp.sum(jnp.where(lane == me, tallied, 0).astype(jnp.float32), axis=1, keepdims=True)
-    owner_ref[...] = jnp.broadcast_to(mine, tallied.shape).astype(jnp.int32)
+    line_of = lax.broadcasted_iota(jnp.int32, tallied.shape, 0)
+    owned = jnp.sum(jnp.where(line_of == lane, mine, 0.0), axis=0, keepdims=True)
+    owner_ref[...] = owned[:, 0:2].astype(jnp.int32)
     for half in range(2):
         mixed = total[half]
         for back in (1, 3):
@@ -725,7 +743,7 @@
     for half in range(2):
         for side in range(2):
             relay(half, side).wait_send()
-    for copy in shards.values():
+    for copy in list(shards.values()) + far_down:
         copy.wait_send()
 
     def settle(step, carry):
@@ -742,7 +760,7 @@
             lend(half, side).wait_send()
 
 
-def moe(rows, table, counts, residual, gate_up, down):
+def moe(rows, table, counts, residual, gate_up, downs):
     any_space = pl.BlockSpec(memory_space=pl.ANY)
     vmem = pl.BlockSpec(memory_space=pltpu.VMEM)
     dma = pltpu.SemaphoreType.DMA
@@ -753,9 +771,9 @@
         moe_kernel,
         out_shape=(
             jax.ShapeDtypeStruct((2 * HALF, WIDTH), bf16),
-            jax.ShapeDtypeStruct((8, 128), jnp.int32),
+            jax.ShapeDtypeStruct((1, 2), jnp.int32),
         ),
-        in_specs=[vmem, vmem, vmem, vmem, any_space, any_space],
+        in_specs=[vmem] * 4 + [any_space] * 5,
         out_specs=(vmem, vmem),
         scratch_shapes=[
             pltpu.VMEM(halves, bf16),
@@ -768,7 +786,7 @@
             pltpu.VMEM(halves, bf16),
             pltpu.VMEM((2, HALF, WIDTH), jnp.float32),
             pltpu.VMEM((2, 8, 96, WIDTH), bf16),
-            pltpu.VMEM((WIDTH, HIDDEN), bf16),
+            pltpu.VMEM((8, 192, HIDDEN), bf16),
             pltpu.VMEM((4, 8, 128), jnp.int32),
             pltpu.VMEM((4, 3, 8, 128), jnp.int32),
             dma((2, SIDE)),
@@ -787,7 +805,9 @@
             dma((SIDE, 2)),
             dma((2, 2)),
             dma((2, 2)),
-            dma(()),
+            dma((SIDE,)),
+            dma((SIDE,)),
+            dma((SIDE,)),
             dma((2, 2)),
             dma((2, 2)),
             pltpu.VMEM((2, 2, HALF // 2, WIDTH), bf16),
@@ -799,7 +819,7 @@
             collective_id=1, has_side_effects=True, vmem_limit_bytes=60 << 20
         ),
         cost_estimate=pl.CostEstimate(flops=17 * 10**9, bytes_accessed=10**7, transcendentals=0),
-    )(rows, table, counts, residual, gate_up, down)
+    )(rows, table, counts, residual, gate_up, *downs)
 
 
 def on_device(
@@ -821,7 +841,11 @@
     w_gate_up,
     w_down,
 ):
-    down = lax.all_gather(w_down, "expert", axis=1, tiled=True)
+    columns = lax.axis_size("expert")
+    downs = [w_down] + [
+        lax.ppermute(w_down, "expert", [(i, (i + 2 * k) % columns) for i in range(columns)])
+        for k in range(1, columns // 2)
+    ]
     residual, normed_mid, table, counts = front(
         tokens,
         attn_gain,
@@ -839,10 +863,9 @@
         route_gate,
         replica_owner,
     )
-    layer_out, owner_counts = moe(
-        normed_mid, table, counts, residual, w_gate_up.transpose(0, 2, 1, 3), down
+    return moe(
+        normed_mid, table, counts, residual, w_gate_up.transpose(0, 2, 1, 3), downs
     )
-    return (layer_out, owner_counts[: w_gate_up.shape[0], 0][None, :])
 
 
 def solution(mesh):

time: 173 us -> 162 us (0.936)
  between operations: 14 us -> 0.7 us
  waiting for transfers between devices: 10.5 us -> 0.01 us
  starting transfers between devices: 0.04 us -> 6.5 us
  Pallas kernels: 143 us -> 148 us
    all_gather x1 -> x0, waiting for transfers between devices: 9.78 us -> none  [on_device(): down = lax.all_gather(w_down, 'expert', axis=1, tiled=True)]
    ppermute x0 -> x3, starting transfers between devices: none -> 6.5 us  [on_device(): lax.ppermute(w_down, 'expert', [(i, (i + 2 * k) % columns) for i in range...]
    pallas_call x1, Pallas kernels: 115 us -> 120 us  [moe(): pl.pallas_call(moe_kernel, out_shape=(jax.ShapeDtypeStruct((2 * HALF, WID...]
    unnamed x2 -> x9, local copies, waits for them, and re-layouts: 4.52 us -> 6.81 us
  transfers between devices with their start and end apart: 1 -> 3, of which waited for: 1 -> 0; matrix products, arithmetic and copies ran while one was open for 1% -> 1% of each run, Pallas kernels for 16% -> 17%
where the time goes in v2:
time: 162 us
  Pallas kernels  148 us (91%)
  local copies, waits for them, and re-layouts  6.81 us (4%)
  starting transfers between devices  6.5 us (4%)
    pallas_call x1, Pallas kernels, moe(): pl.pallas_call(moe_kernel, out_shape=(jax.ShapeDtypeStruct((2 * HALF, WID...  120 us
    pallas_call x1, Pallas kernels, front(): pl.pallas_call(front_kernel, out_shape=(jax.ShapeDtypeStruct((count, widt...  27.6 us
    unnamed x9, local copies, waits for them, and re-layouts  6.81 us
    ppermute x3, starting transfers between devices, on_device(): lax.ppermute(w_down, 'expert', [(i, (i + 2 * k) % columns) for i in range...  6.5 us
  transfers between devices with their start and end apart: 3, of which 0 were waited for; matrix products, arithmetic and copies ran while one was open for 1% of the time, Pallas kernels for 17%

profile of v2, /device:TPU:1, one launch (start us, length us, event | category | flops | bytes accessed | tf_op | source)
XLA Modules:
  0.0 162.1 jit_solution(9081011672412421380)
XLA Ops:
  0.6 3.8 %collective-permute-start.1 = (bf16[2,192,768]{2,1,0:T(8,128)(2,1)}, bf16[2,192,768]{2,1,0:T(8,128)(2,1)S(1)}, u32[]{:S(2)}, u32[]{:S(2)}) collective-permute-start(bf16[2,192,768]{2,1,0:T(8,128)(2,1)} %down_a.1), channel_id=1, source_target_pairs={{0,4},{1,5},{2,6},{3,7},{4,0},{5,1},{6,2},{7,3},{8,12},{9,13},{10,... | collective-permute-start | bytes 1769480 | tf_op jit(solution)/shard_map/ppermute | solution.py:846
  4.5 0.4 collective-permute-start
  4.9 2.3 %collective-permute-start.2 = (bf16[2,192,768]{2,1,0:T(8,128)(2,1)}, bf16[2,192,768]{2,1,0:T(8,128)(2,1)S(1)}, u32[]{:S(2)}, u32[]{:S(2)}) collective-permute-start(bf16[2,192,768]{2,1,0:T(8,128)(2,1)} %down_a.1), channel_id=1, source_target_pairs={{0,6},{1,7},{2,0},{3,1},{4,2},{5,3},{6,4},{7,5},{8,14},{9,15},{10,... | collective-permute-start | bytes 1769480 | tf_op jit(solution)/shard_map/ppermute | solution.py:846
  7.1 2.4 %copy.22 = bf16[2,96,2,1536]{3,1,2,0:T(8,128)(2,1)} copy(bf16[2,96,2,1536]{3,2,1,0:T(2,128)(2,1)} %param.33) | data formatting | bytes 2359296 | tf_op args[15]
  9.6 27.6 %front.1 = (bf16[256,1536]{1,0:T(8,128)(2,1)}, bf16[256,1536]{1,0:T(8,128)(2,1)}, f32[8,256]{1,0:T(8,128)}, s32[8,128]{1,0:T(8,128)}) custom-call(s32[1,3]{1,0:T(1,128)} %lengths_ref.1, s32[1,3]{1,0:T(1,128)} %cached_ref.1, s32[1,8]{1,0:T(1,128)} %pick_ref.1, bf16[256,1536]{1,0:T(8,128)(2,1)} %tokens_ref.1, f32[1536]{0:T(1024)} %attn_gain_ref.1, ...), custom_call_target="tpu_custom_call" | custom-call | flops 12000000000 | bytes 60000000 | tf_op jit(solution)/shard_map/front/pallas_call | solution.py:282
  37.1 0.0 collective-permute-done.1.down_c
  37.1 0.0 copy-start
  37.1 0.0 collective-permute-done.down_b
  37.2 0.0 copy-start.1
  37.2 0.0 collective-permute-done.2.down_d
  37.2 0.0 copy-start.2
  37.2 0.8 copy-done
  38.0 0.2 copy-done.1
  38.1 0.2 copy-done.2
  38.3 120.5 %moe.1 = (bf16[256,1536]{1,0:T(8,128)(2,1)}, s32[1,2]{1,0:T(1,128)}) custom-call(bf16[256,1536]{1,0:T(8,128)(2,1)} %get-tuple-element.6.rows_ref, f32[8,256]{1,0:T(8,128)} %get-tuple-element.7.table_ref, s32[8,128]{1,0:T(8,128)} %get-tuple-element.8.counts_ref, bf16[256,1536]{1,0:T(8,128)(2,1)} %get-tuple-element.9.residual_ref, ...), custom_call_target="tpu_custom_call" | custom-call | flops 16999999488 | bytes 10000000 | tf_op jit(solution)/shard_map/moe/pallas_call | solution.py:770
  158.8 2.1 %copy.25 = bf16[256,1536]{1,0:T(8,128)(2,1)} copy(bf16[256,1536]{1,0:T(8,128)(2,1)} %get-tuple-element.12) | data formatting | bytes 1572864
  160.9 1.2 copy.26
Async XLA Ops:
  0.6 36.5 %collective-permute-start.1 = (bf16[2,192,768]{2,1,0:T(8,128)(2,1)}, bf16[2,192,768]{2,1,0:T(8,128)(2,1)S(1)}, u32[]{:S(2)}, u32[]{:S(2)}) collective-permute-start(bf16[2,192,768]{2,1,0:T(8,128)(2,1)} %down_a.1), channel_id=1, source_target_pairs={{0,4},{1,5},{2,6},{3,7},{4,0},{5,1},{6,2},{7,3},{8,12},{9,13},{10,... | collective-permute-start | bytes 1769480 | tf_op jit(solution)/shard_map/ppermute | solution.py:846
  4.5 32.7 %collective-permute-start = (bf16[2,192,768]{2,1,0:T(8,128)(2,1)}, bf16[2,192,768]{2,1,0:T(8,128)(2,1)S(1)}, u32[]{:S(2)}, u32[]{:S(2)}) collective-permute-start(bf16[2,192,768]{2,1,0:T(8,128)(2,1)} %down_a.1), channel_id=1, source_target_pairs={{0,2},{1,3},{2,4},{3,5},{4,6},{5,7},{6,0},{7,1},{8,10},{9,11},{10,... | collective-permute-start | bytes 1769480 | tf_op jit(solution)/shard_map/ppermute | solution.py:846
  4.9 32.3 %collective-permute-start.2 = (bf16[2,192,768]{2,1,0:T(8,128)(2,1)}, bf16[2,192,768]{2,1,0:T(8,128)(2,1)S(1)}, u32[]{:S(2)}, u32[]{:S(2)}) collective-permute-start(bf16[2,192,768]{2,1,0:T(8,128)(2,1)} %down_a.1), channel_id=1, source_target_pairs={{0,6},{1,7},{2,0},{3,1},{4,2},{5,3},{6,4},{7,5},{8,14},{9,15},{10,... | collective-permute-start | bytes 1769480 | tf_op jit(solution)/shard_map/ppermute | solution.py:846
  37.1 0.8 copy-start
  37.2 1.0 copy-start.1
  37.2 1.2 copy-start.2

commit v3 on v2

--- a/solution.py
+++ b/solution.py
@@ -635,8 +635,7 @@
     last = (((1,), (1,)), ((), ()))
 
     def serve(step, carry):
-        turn_at = step // 2
-        half, back = step % 2, 2 - turn_at + 3 * (turn_at // 2) - 2 * (turn_at // 3)
+        half, back = step % 2, step // 2
         for copy in copies_out(half, back):
             copy.wait()
         arrived = landed[half, back].reshape(CHUNK, WIDTH)

time: 162 us -> 158 us (0.975); the launches traced: 162 us -> 156 us
  Pallas kernels: 148 us -> 142 us
    pallas_call x1, Pallas kernels: 120 us -> 114 us  [moe(): pl.pallas_call(moe_kernel, out_shape=(jax.ShapeDtypeStruct((2 * HALF, WID...]
  transfers between devices with their start and end apart: 3 -> 3, of which waited for: 0 -> 0; matrix products, arithmetic and copies ran while one was open for 1% -> 2% of each run, Pallas kernels for 17% -> 18%
where the time goes in v3:
time: 158 us; the launch traced here: 156 us
  Pallas kernels  142 us (90%)
  local copies, waits for them, and re-layouts  6.81 us (4%)
  starting transfers between devices  6.5 us (4%)
    pallas_call x1, Pallas kernels, moe(): pl.pallas_call(moe_kernel, out_shape=(jax.ShapeDtypeStruct((2 * HALF, WID...  114 us
    pallas_call x1, Pallas kernels, front(): pl.pallas_call(front_kernel, out_shape=(jax.ShapeDtypeStruct((count, widt...  27.6 us
    unnamed x9, local copies, waits for them, and re-layouts  6.81 us
    ppermute x3, starting transfers between devices, on_device(): lax.ppermute(w_down, 'expert', [(i, (i + 2 * k) % columns) for i in range...  6.5 us
  transfers between devices with their start and end apart: 3, of which 0 were waited for; matrix products, arithmetic and copies ran while one was open for 2% of the time, Pallas kernels for 18%

profile of v3, /device:TPU:1, one launch (start us, length us, event | category | flops | bytes accessed | tf_op | source)
XLA Modules:
  0.0 155.6 jit_solution(7838528971179906485)
XLA Ops:
  0.6 3.8 %collective-permute-start.1 = (bf16[2,192,768]{2,1,0:T(8,128)(2,1)}, bf16[2,192,768]{2,1,0:T(8,128)(2,1)S(1)}, u32[]{:S(2)}, u32[]{:S(2)}) collective-permute-start(bf16[2,192,768]{2,1,0:T(8,128)(2,1)} %down_a.1), channel_id=1, source_target_pairs={{0,4},{1,5},{2,6},{3,7},{4,0},{5,1},{6,2},{7,3},{8,12},{9,13},{10,... | collective-permute-start | bytes 1769480 | tf_op jit(solution)/shard_map/ppermute | solution.py:845
  4.5 0.4 collective-permute-start
  4.9 2.3 %collective-permute-start.2 = (bf16[2,192,768]{2,1,0:T(8,128)(2,1)}, bf16[2,192,768]{2,1,0:T(8,128)(2,1)S(1)}, u32[]{:S(2)}, u32[]{:S(2)}) collective-permute-start(bf16[2,192,768]{2,1,0:T(8,128)(2,1)} %down_a.1), channel_id=1, source_target_pairs={{0,6},{1,7},{2,0},{3,1},{4,2},{5,3},{6,4},{7,5},{8,14},{9,15},{10,... | collective-permute-start | bytes 1769480 | tf_op jit(solution)/shard_map/ppermute | solution.py:845
  7.1 2.4 %copy.22 = bf16[2,96,2,1536]{3,1,2,0:T(8,128)(2,1)} copy(bf16[2,96,2,1536]{3,2,1,0:T(2,128)(2,1)} %param.33) | data formatting | bytes 2359296 | tf_op args[15]
  9.6 27.6 %front.1 = (bf16[256,1536]{1,0:T(8,128)(2,1)}, bf16[256,1536]{1,0:T(8,128)(2,1)}, f32[8,256]{1,0:T(8,128)}, s32[8,128]{1,0:T(8,128)}) custom-call(s32[1,3]{1,0:T(1,128)} %lengths_ref.1, s32[1,3]{1,0:T(1,128)} %cached_ref.1, s32[1,8]{1,0:T(1,128)} %pick_ref.1, bf16[256,1536]{1,0:T(8,128)(2,1)} %tokens_ref.1, f32[1536]{0:T(1024)} %attn_gain_ref.1, ...), custom_call_target="tpu_custom_call" | custom-call | flops 12000000000 | bytes 60000000 | tf_op jit(solution)/shard_map/front/pallas_call | solution.py:282
  37.1 0.0 collective-permute-done.1.down_c
  37.1 0.0 copy-start
  37.1 0.0 collective-permute-done.down_b
  37.2 0.0 copy-start.1
  37.2 0.0 collective-permute-done.2.down_d
  37.2 0.0 copy-start.2
  37.2 0.8 copy-done
  38.0 0.2 copy-done.1
  38.1 0.2 copy-done.2
  38.3 114.0 %moe.1 = (bf16[256,1536]{1,0:T(8,128)(2,1)}, s32[1,2]{1,0:T(1,128)}) custom-call(bf16[256,1536]{1,0:T(8,128)(2,1)} %get-tuple-element.6.rows_ref, f32[8,256]{1,0:T(8,128)} %get-tuple-element.7.table_ref, s32[8,128]{1,0:T(8,128)} %get-tuple-element.8.counts_ref, bf16[256,1536]{1,0:T(8,128)(2,1)} %get-tuple-element.9.residual_ref, ...), custom_call_target="tpu_custom_call" | custom-call | flops 16999999488 | bytes 10000000 | tf_op jit(solution)/shard_map/moe/pallas_call | solution.py:769
  152.3 2.1 %copy.25 = bf16[256,1536]{1,0:T(8,128)(2,1)} copy(bf16[256,1536]{1,0:T(8,128)(2,1)} %get-tuple-element.12) | data formatting | bytes 1572864
  154.4 1.2 copy.26
Async XLA Ops:
  0.6 36.5 %collective-permute-start.1 = (bf16[2,192,768]{2,1,0:T(8,128)(2,1)}, bf16[2,192,768]{2,1,0:T(8,128)(2,1)S(1)}, u32[]{:S(2)}, u32[]{:S(2)}) collective-permute-start(bf16[2,192,768]{2,1,0:T(8,128)(2,1)} %down_a.1), channel_id=1, source_target_pairs={{0,4},{1,5},{2,6},{3,7},{4,0},{5,1},{6,2},{7,3},{8,12},{9,13},{10,... | collective-permute-start | bytes 1769480 | tf_op jit(solution)/shard_map/ppermute | solution.py:845
  4.5 32.7 %collective-permute-start = (bf16[2,192,768]{2,1,0:T(8,128)(2,1)}, bf16[2,192,768]{2,1,0:T(8,128)(2,1)S(1)}, u32[]{:S(2)}, u32[]{:S(2)}) collective-permute-start(bf16[2,192,768]{2,1,0:T(8,128)(2,1)} %down_a.1), channel_id=1, source_target_pairs={{0,2},{1,3},{2,4},{3,5},{4,6},{5,7},{6,0},{7,1},{8,10},{9,11},{10,... | collective-permute-start | bytes 1769480 | tf_op jit(solution)/shard_map/ppermute | solution.py:845
  4.9 32.3 %collective-permute-start.2 = (bf16[2,192,768]{2,1,0:T(8,128)(2,1)}, bf16[2,192,768]{2,1,0:T(8,128)(2,1)S(1)}, u32[]{:S(2)}, u32[]{:S(2)}) collective-permute-start(bf16[2,192,768]{2,1,0:T(8,128)(2,1)} %down_a.1), channel_id=1, source_target_pairs={{0,6},{1,7},{2,0},{3,1},{4,2},{5,3},{6,4},{7,5},{8,14},{9,15},{10,... | collective-permute-start | bytes 1769480 | tf_op jit(solution)/shard_map/ppermute | solution.py:845
  37.1 0.8 copy-start
  37.2 1.0 copy-start.1
  37.2 1.2 copy-start.2
